TPU v7x, 768 devices: a whole 4x8x12 slice. The times are simulated.
768 devices in a mesh: dam: 128 (over x, z_lo, y), sec: 6 (over z_hi, core).
Axes of the slice: x: 4, y: 8, z: 12 (z_hi: 3, z_lo: 4; z = z_hi * 4 + z_lo), core: 2. Of those that a mesh axis runs over, the one named last changes fastest.
Arguments:
- segment_load: float32 [128, 6, 16, 1024], P('dam', 'sec')
- segment_mask: int32 [128, 6, 16, 16], P('dam', 'sec'), may hold values 0 or 1
- stiffness: float32 [128, 6, 16, 64, 448], P('dam', 'sec'), may hold values from -2 to 3, as said below
- block_cols: int32 [128, 6, 16, 7], P('dam', 'sec'), may hold values from 0 to 15, as said below
- capillary: float32 [128, 6, 16, 64], P('dam', 'sec'), may hold values from 0.25 to 2
- dirichlet_blocks: float32 [128, 6, 16, 64, 64], P('dam', 'sec'), may hold values from -1 to 1, as said below
- face_map: int32 [128, 6, 4, 8], P('dam', 'sec'), may hold values from 0 to 15, as said below
- face_weight: float32 [128, 6, 4, 512], P('dam', 'sec'), may hold values from 0 to 2, as said below
- corner_map: int32 [128, 6, 4], P('dam', 'sec'), may hold values from 0 to 15, as said below
- coarse_inverse: float32 [128, 1536, 1536], P('dam', 'sec'), may hold values from -1 to 1, as said below
Outputs:
- solution: float32 [128, 6, 16, 1024], P('dam', 'sec')
- residual: float32 [128, 6, 16, 1024], P('dam', 'sec')
Inputs may be any that keep to these rules, and one draw needn't show every extreme that they name: `block_cols`: in each subdomain block b stores blocks b, b + o1, b - o1, b + o2, b - o2, b + o3, b - o3 (mod 16), for 3 distinct offsets o1, o2, o3 from 1 to 7 drawn per subdomain, in that order. The stiffness is symmetric, its off-diagonal entries of a row sum in magnitude to under 1.5, and its diagonal entries are 2 to 3. `dirichlet_blocks`: each block is symmetric and positive definite. `coarse_inverse`: each cross-section's matrix is symmetric and positive definite. `face_map`: the 8 blocks of a face are distinct; position p of a face meets position p of the neighbour's opposite face. `face_weight`: equal on the two sides of an interface, zero on faces with no neighbour. `corner_map`: distinct within a subdomain.
All inputs are finite; a program needn't handle non-finite values. No bound on the sum of `segment_mask` on one device may be relied on, other than what follows from the above.
Results may differ from a plain program's by a relative error of at most 0.00075.
Values sent between devices are 32-bit elements; how exact they have to be, the bound alone decides.
A program may use at most 32 MiB of HBM per device.

v0:
```python
import jax
import jax.numpy as jnp
from jax import lax
from jax.sharding import PartitionSpec as P

ITERS = 2


HIGH = lax.Precision.HIGHEST


def with_halo(array, sides, width):
    for axis, dim in sides:
        peers, length = (lax.axis_size(axis), array.shape[dim])
        up = [(i, (i + 1) % peers) for i in range(peers - 1)]
        down = [(j, i) for i, j in up]
        last = lax.slice_in_dim(array, length - width, length, axis=dim)
        first = lax.slice_in_dim(array, 0, width, axis=dim)
        before = lax.ppermute(last, axis, up)
        after = lax.ppermute(first, axis, down)
        array = jnp.concatenate([before, array, after], axis=dim)
    return array


def local_product(stiff, cols, tang, field):
    nblk, bdof = tang.shape
    ncol = field.shape[1] // bdof
    gathered = field[cols].reshape(nblk, cols.shape[1] * bdof, ncol)
    prod = jnp.einsum("bde,bes->bds", stiff, gathered, precision=HIGH)
    prod = prod + tang[:, :, None] * field.reshape(nblk, bdof, ncol)
    return prod.reshape(nblk, bdof * ncol)


def shards(
    segment_load,
    segment_mask,
    stiffness,
    block_cols,
    capillary,
    dirichlet_blocks,
    face_map,
    face_weight,
    corner_map,
    coarse_inverse,
):
    stiff = stiffness[0, 0]
    cols = block_cols[0, 0]
    tang = capillary[0, 0]
    blocks_pre = dirichlet_blocks[0, 0]
    fmap = face_map[0, 0]
    cmap = corner_map[0, 0]
    own_rows = coarse_inverse[0]
    nblk, bdof = tang.shape
    width = segment_load.shape[-1]
    ncol = width // bdof
    nface = fmap.shape[1]
    ncorner = cmap.shape[0]
    weights = face_weight[0, 0].reshape(4, nface, bdof, 1)
    flat_faces = fmap.reshape(4 * nface)
    masked = (
        segment_load[0, 0].reshape(nblk, bdof, ncol)
        * segment_mask[0, 0].astype(jnp.float32)[:, None, :]
    )
    resid = masked.reshape(nblk, width)

    def precondition(field):
        outz = jnp.einsum(
            "bde,bes->bds", blocks_pre, field.reshape(nblk, bdof, ncol), precision=HIGH
        ).reshape(nblk, width)
        corners = field[cmap]
        piece = lax.all_gather(corners, "sec", axis=0, tiled=True)
        correct = jnp.dot(
            own_rows, piece.reshape(piece.shape[0] * bdof, ncol), precision=HIGH
        ).reshape(ncorner, width)
        return outz.at[cmap].add(correct)

    def inner(first, second):
        return (first * second).reshape(nblk, bdof, ncol).sum(axis=(0, 1))

    def spread(coef):
        return jnp.tile(coef, bdof)

    def global_inner(first, second):
        return lax.psum(inner(first, second), ("dam", "sec"))

    solution = jnp.zeros_like(resid)
    zvec = precondition(resid)
    direction = zvec
    gamma = global_inner(resid, zvec)
    for step in range(ITERS):
        local = local_product(stiff, cols, tang, direction)
        faces = direction[fmap]
        dam_side = with_halo(faces[0:2], (("dam", 0),), 1)
        sec_side = with_halo(faces[2:4], (("sec", 0),), 1)
        beside = jnp.stack([dam_side[0], dam_side[3], sec_side[0], sec_side[3]])
        term = (weights * (faces - beside).reshape(4, nface, bdof, ncol)).reshape(4 * nface, width)
        image = local.at[flat_faces].add(term)
        delta = global_inner(direction, image)
        alpha = spread(gamma / delta)
        solution = solution + alpha * direction
        resid = resid - alpha * image
        if step + 1 < ITERS:
            zvec = precondition(resid)
            gnew = global_inner(resid, zvec)
            direction = zvec + spread(gnew / gamma) * direction
            gamma = gnew
    return (solution[None, None], resid[None, None])


def solution(mesh):
    placed = (
        P("dam", "sec", None, None),
        P("dam", "sec", None, None),
        P("dam", "sec", None, None, None),
        P("dam", "sec", None, None),
        P("dam", "sec", None, None),
        P("dam", "sec", None, None, None),
        P("dam", "sec", None, None),
        P("dam", "sec", None, None),
        P("dam", "sec", None),
        P("dam", "sec", None),
    )
    return jax.shard_map(
        shards,
        mesh=mesh,
        in_specs=placed,
        out_specs=(P("dam", "sec", None, None), P("dam", "sec", None, None)),
        check_vma=False,
    )
```

profile of v0, /device:TPU:1, one launch (start us, length us, event | category | flops | bytes accessed | tf_op | source)
XLA Modules:
  0.0 465.7 jit_solution(12477808821921786068)
XLA Ops:
  5.8 24.7 %all-gather.2 = f32[6,4,1024]{2,1,0:T(4,128)S(1)} all-gather(f32[1,4,1024]{2,1,0:T(4,128)S(1)} %bitcast.98), channel_id=2, replica_groups=mesh['dam'=128,'sec'=6] {'sec'}, dimensions={0}, use_global_device_ids=true | all-gather | bytes 114688 | tf_op jit(solution)/shard_map/all_gather | solution.py:71
  30.8 2.8 fusion.20
  35.9 2.1 collective-permute-start.3
  38.0 7.4 %collective-permute-start.2 = (f32[1,8,1024]{2,1,0:T(8,128)}, f32[1,8,1024]{2,1,0:T(8,128)}, u32[]{:S(2)}, u32[]{:S(2)}) collective-permute-start(f32[1,8,1024]{2,1,0:T(8,128)} %get-tuple-element.11), channel_id=1, source_target_pairs={{0,1},{1,2},{2,3},{3,4},{4,5},{6,7},{7,8},{8,9},{9,10},{10,11},{12... | collective-permute-start | bytes 98312 | tf_op jit(solution)/shard_map/ppermute | solution.py:19
  46.7 4.6 collective-permute-start
  52.5 3.0 reshape.203
  55.8 7.9 %fusion.11 = f32[16,64,16]{1,2,0:T(8,128)S(1)} fusion(f32[16,448,16]{2,1,0:T(8,128)} %reshape.203, f32[1,1,16,64,448]{4,3,2,1,0:T(8,128)S(1)} %copy-done, f32[16,64,16]{1,2,0:T(8,128)S(1)} %copy.59, f32[16,64]{1,0:T(8,128)S(1)} %bitcast.99), kind=kOutput, calls=%fused_computation.21 | convolution fusion | flops 88113152 | bytes 2428928 | tf_op jit(solution)/shard_map/bde,bes->bds/dot_general | solution.py:29
  66.4 1.6 stack.29
  67.9 1.6 stack.28
  69.5 1.6 stack.27
  71.1 1.6 stack.26
  75.2 2.7 scatter_custom_fusion.1
  79.0 112.7 %all-reduce = (f32[16]{0:T(128)S(1)}, f32[16]{0:T(128)S(1)}) all-reduce(f32[16]{0:T(128)S(1)} %reduce_sum.51, f32[16]{0:T(128)S(1)} %reduce_sum.54), channel_id=1, replica_groups=mesh['dam'=128,'sec'=6] {'dam','sec'}, use_global_device_ids=true, to_apply=%region_3.0 | all-reduce | flops 32 | bytes 256 | tf_op jit(solution)/shard_map/psum | solution.py:84
  193.6 1.6 convolution_bitcast_fusion
  196.6 14.9 %all-gather.3 = f32[6,4,1024]{2,1,0:T(4,128)S(1)} all-gather(f32[1,4,1024]{2,1,0:T(4,128)S(1)} %bitcast.97), channel_id=3, replica_groups=mesh['dam'=128,'sec'=6] {'sec'}, dimensions={0}, use_global_device_ids=true | all-gather | bytes 114688 | tf_op jit(solution)/shard_map/all_gather | solution.py:71
  211.9 2.8 fusion.23
  215.7 104.3 %psum.30 = f32[16]{0:T(128)S(1)} all-reduce(f32[16]{0:T(128)S(1)} %reduce_sum.72), channel_id=1, replica_groups=mesh['dam'=128,'sec'=6] {'dam','sec'}, use_global_device_ids=true, to_apply=%region_11.0 | all-reduce | flops 16 | bytes 128 | tf_op jit(solution)/shard_map/psum | solution.py:84
  322.4 3.0 reshape.210
  326.3 2.6 collective-permute-start.7
  328.9 6.9 %collective-permute-start.6 = (f32[1,8,1024]{2,1,0:T(8,128)}, f32[1,8,1024]{2,1,0:T(8,128)S(1)}, u32[]{:S(2)}, u32[]{:S(2)}) collective-permute-start(f32[1,8,1024]{2,1,0:T(8,128)} %get-tuple-element.7), channel_id=1, source_target_pairs={{0,1},{1,2},{2,3},{3,4},{4,5},{6,7},{7,8},{8,9},{9,10},{10,11},{12... | collective-permute-start | bytes 98312 | tf_op jit(solution)/shard_map/ppermute | solution.py:19
  337.1 4.0 collective-permute-start.4
  341.1 7.9 %fusion.17 = f32[16,64,16]{1,2,0:T(8,128)S(1)} fusion(f32[16,448,16]{2,1,0:T(8,128)} %reshape.210, f32[1,1,16,64,448]{4,3,2,1,0:T(8,128)S(1)} %copy-done, f32[16,64,16]{1,2,0:T(8,128)S(1)} %copy.65, f32[16,64]{1,0:T(8,128)S(1)} %bitcast.100), kind=kOutput, calls=%fused_computation.23 | convolution fusion | flops 88113152 | bytes 2428928 | tf_op jit(solution)/shard_map/bde,bes->bds/dot_general | solution.py:29
  355.3 1.3 scatter_custom_fusion.3
  356.8 108.2 %psum.31 = f32[16]{0:T(128)S(1)} all-reduce(f32[16]{0:T(128)S(1)} %reduce_sum.75), channel_id=1, replica_groups=mesh['dam'=128,'sec'=6] {'dam','sec'}, use_global_device_ids=true, to_apply=%region_15.16 | all-reduce | flops 16 | bytes 128 | tf_op jit(solution)/shard_map/psum | solution.py:84
  (120 shorter events, 32.9 us)
Async XLA Ops:
  0.6 55.1 %copy-start = (f32[1,1,16,64,448]{4,3,2,1,0:T(8,128)S(1)}, f32[1,1,16,64,448]{4,3,2,1,0:T(8,128)}, u32[]{:S(2)}) copy-start(f32[1,1,16,64,448]{4,3,2,1,0:T(8,128)} %param.12) | copy-start | bytes 5505028
  0.6 3.1 copy-start.1
  1.5 3.7 copy-start.12
  4.9 28.9 %copy-start.7 = (s32[1,1,4,8]{3,2,1,0:T(4,128)S(1)}, s32[1,1,4,8]{3,2,1,0:T(4,128)}, u32[]{:S(2)}) copy-start(s32[1,1,4,8]{3,2,1,0:T(4,128)} %param.16) | copy-start | bytes 388
  5.2 30.0 %copy-start.9 = (s32[4]{0:T(128)}, s32[4]{0:T(128)S(1)}, u32[]{:S(2)}) copy-start(s32[4]{0:T(128)S(1)} %fusion.36) | copy-start | bytes 52
  5.2 25.5 %copy-start.8 = (s32[1024]{0:T(1024)}, s32[1024]{0:T(1024)S(1)}, u32[]{:S(2)}) copy-start(s32[1024]{0:T(1024)S(1)} %pad_clamp_fusion.2) | copy-start | bytes 12292
  30.8 20.8 %copy-start.11 = (s32[1,1,16,7]{2,1,3,0:T(1,128)S(1)}, s32[1,1,16,7]{2,1,3,0:T(1,128)}, u32[]{:S(2)}) copy-start(s32[1,1,16,7]{2,1,3,0:T(1,128)} %param.13) | copy-start | bytes 1348
  33.9 17.6 %copy-start.5 = (s32[1024]{0:T(1024)}, s32[1024]{0:T(1024)S(1)}, u32[]{:S(2)}) copy-start(s32[1024]{0:T(1024)S(1)} %pad_clamp_fusion) | copy-start | bytes 12292
  35.9 30.5 %collective-permute-start.3 = (f32[1,8,1024]{2,1,0:T(8,128)}, f32[1,8,1024]{2,1,0:T(8,128)}, u32[]{:S(2)}, u32[]{:S(2)}) collective-permute-start(f32[1,8,1024]{2,1,0:T(8,128)} %get-tuple-element.13), channel_id=1, source_target_pairs={{1,0},{2,1},{3,2},{4,3},{5,4},{7,6},{8,7},{9,8},{10,9},{11,10},{13... | collective-permute-start | bytes 98312 | tf_op jit(solution)/shard_map/ppermute | solution.py:20
  38.0 30.0 %collective-permute-start.2 = (f32[1,8,1024]{2,1,0:T(8,128)}, f32[1,8,1024]{2,1,0:T(8,128)}, u32[]{:S(2)}, u32[]{:S(2)}) collective-permute-start(f32[1,8,1024]{2,1,0:T(8,128)} %get-tuple-element.11), channel_id=1, source_target_pairs={{0,1},{1,2},{2,3},{3,4},{4,5},{6,7},{7,8},{8,9},{9,10},{10,11},{12... | collective-permute-start | bytes 98312 | tf_op jit(solution)/shard_map/ppermute | solution.py:19
  45.4 24.2 %collective-permute-start.1 = (f32[1,8,1024]{2,1,0:T(8,128)}, f32[1,8,1024]{2,1,0:T(8,128)}, u32[]{:S(2)}, u32[]{:S(2)}) collective-permute-start(f32[1,8,1024]{2,1,0:T(8,128)} %get-tuple-element.12), channel_id=1, source_target_pairs={{6,0},{12,6},{18,12},{24,18},{30,24},{36,30},{42,36},{48,42},{54,4... | collective-permute-start | bytes 98312 | tf_op jit(solution)/shard_map/ppermute | solution.py:20
  46.7 24.5 %collective-permute-start = (f32[1,8,1024]{2,1,0:T(8,128)}, f32[1,8,1024]{2,1,0:T(8,128)}, u32[]{:S(2)}, u32[]{:S(2)}) collective-permute-start(f32[1,8,1024]{2,1,0:T(8,128)} %get-tuple-element.10), channel_id=1, source_target_pairs={{0,6},{6,12},{12,18},{18,24},{24,30},{30,36},{36,42},{42,48},{48,5... | collective-permute-start | bytes 98312 | tf_op jit(solution)/shard_map/ppermute | solution.py:19
  52.5 3.2 copy-start.4
  55.8 9.6 %copy-start.6 = (f32[1,1,4,512]{3,2,1,0:T(4,128)S(1)}, f32[1,1,4,512]{3,2,1,0:T(4,128)}, u32[]{:S(2)}) copy-start(f32[1,1,4,512]{3,2,1,0:T(4,128)} %param.17) | copy-start | bytes 24580
  75.2 118.4 %copy-start.2 = (f32[1,1,16,64,64]{4,3,2,1,0:T(8,128)S(1)}, f32[1,1,16,64,64]{4,3,2,1,0:T(8,128)}, u32[]{:S(2)}) copy-start(f32[1,1,16,64,64]{4,3,2,1,0:T(8,128)} %param.15) | copy-start | bytes 786436
  196.4 18.5 %copy-start.10 = (s32[4]{0:T(128)S(1)}, s32[4]{0:T(128)}, u32[]{:S(2)}) copy-start(s32[4]{0:T(128)} %copy-done.9) | copy-start | bytes 52
  320.0 0.6 copy-start.13
  322.4 3.2 copy-start.3
  326.3 23.1 %collective-permute-start.7 = (f32[1,8,1024]{2,1,0:T(8,128)}, f32[1,8,1024]{2,1,0:T(8,128)S(1)}, u32[]{:S(2)}, u32[]{:S(2)}) collective-permute-start(f32[1,8,1024]{2,1,0:T(8,128)} %get-tuple-element.9), channel_id=1, source_target_pairs={{1,0},{2,1},{3,2},{4,3},{5,4},{7,6},{8,7},{9,8},{10,9},{11,10},{13... | collective-permute-start | bytes 98312 | tf_op jit(solution)/shard_map/ppermute | solution.py:20
  328.9 21.4 %collective-permute-start.6 = (f32[1,8,1024]{2,1,0:T(8,128)}, f32[1,8,1024]{2,1,0:T(8,128)S(1)}, u32[]{:S(2)}, u32[]{:S(2)}) collective-permute-start(f32[1,8,1024]{2,1,0:T(8,128)} %get-tuple-element.7), channel_id=1, source_target_pairs={{0,1},{1,2},{2,3},{3,4},{4,5},{6,7},{7,8},{8,9},{9,10},{10,11},{12... | collective-permute-start | bytes 98312 | tf_op jit(solution)/shard_map/ppermute | solution.py:19
  335.8 15.3 %collective-permute-start.5 = (f32[1,8,1024]{2,1,0:T(8,128)S(1)}, f32[1,8,1024]{2,1,0:T(8,128)S(1)}, u32[]{:S(2)}, u32[]{:S(2)}) collective-permute-start(f32[1,8,1024]{2,1,0:T(8,128)S(1)} %get-tuple-element.8), channel_id=1, source_target_pairs={{6,0},{12,6},{18,12},{24,18},{30,24},{36,30},{42,36},{48,42},{54,4... | collective-permute-start | bytes 98312 | tf_op jit(solution)/shard_map/ppermute | solution.py:20
  337.1 14.9 %collective-permute-start.4 = (f32[1,8,1024]{2,1,0:T(8,128)S(1)}, f32[1,8,1024]{2,1,0:T(8,128)S(1)}, u32[]{:S(2)}, u32[]{:S(2)}) collective-permute-start(f32[1,8,1024]{2,1,0:T(8,128)S(1)} %get-tuple-element.6), channel_id=1, source_target_pairs={{0,6},{6,12},{12,18},{18,24},{24,30},{30,36},{36,42},{42,48},{48,5... | collective-permute-start | bytes 98312 | tf_op jit(solution)/shard_map/ppermute | solution.py:19
  351.9 113.0 %copy-start.14 = (f32[16]{0:T(128)S(1)}, f32[16]{0:T(128)}, u32[]{:S(2)}) copy-start(f32[16]{0:T(128)} %copy-done.13) | copy-start | bytes 196
where the time goes:
time: 467 us; the launch traced here: 466 us
  blocking collectives  365 us (78%)
  local copies, waits for them, and re-layouts  33 us (7%)
  starting transfers between devices  30.1 us (6%)
  matrix products  23.9 us (5%)
  other arithmetic  12.8 us (3%)
    psum x3, blocking collectives, global_inner(): return lax.psum(inner(first, second), ('dam', 'sec'))  325 us
    all_gather x2, blocking collectives, precondition(): piece = lax.all_gather(corners, 'sec', axis=0, tiled=True)  39.6 us
    ppermute x4, starting transfers between devices, with_halo(): before = lax.ppermute(last, axis, up)  22.9 us
    dot_general x2, matrix products, local_product(): prod = jnp.einsum('bde,bes->bds', stiff, gathered, precision=HIGH)  15.7 us
    another operation x10, local copies, waits for them, and re-layouts, shards(): beside = jnp.stack([dam_side[0], dam_side[3], sec_side[0], sec_side[3]])  12.2 us
  transfers between devices with their start and end apart: 8, of which 0 were waited for; matrix products, arithmetic and copies ran while one was open for 7% of the time, Pallas kernels for 0%

commit v1 on v0

v1 whole, which is shorter than its diff:
```python
import functools

import jax
import jax.numpy as jnp
from jax import lax
from jax.experimental import pallas as pl
from jax.experimental.pallas import tpu as pltpu
from jax.sharding import PartitionSpec as P

MESH = pl.DeviceIdType.MESH
f32, bf16, i32 = jnp.float32, jnp.bfloat16, jnp.int32
HIGH = lax.Precision.HIGHEST

SPLITS = {128: (4, 4, 8), 8: (2, 2, 2), 4: (1, 2, 2), 2: (1, 1, 2)}


def iota(shape, dim):
    return lax.broadcasted_iota(i32, shape, dim)


def split(a):
    hi = a.astype(bf16)
    return hi, (a - hi.astype(f32)).astype(bf16)


def nn(a, b):
    return jnp.dot(a, b, preferred_element_type=f32)


def nt(a, b, precision=None):
    return lax.dot_general(
        a, b, (((1,), (1,)), ((), ())), precision=precision, preferred_element_type=f32
    )


def roll(a, amount, axis):
    return pltpu.roll(a, amount % a.shape[axis], axis)


def swap8(tile):
    sub, grp = iota((8, 128), 0), iota((8, 128), 1) // 16
    for s in (1, 2, 4):
        up = roll(roll(tile, 16 * s, 1), -s, 0)
        down = roll(roll(tile, -16 * s, 1), s, 0)
        tile = jnp.where(((sub ^ grp) & s) == 0, tile, jnp.where((grp & s) != 0, up, down))
    return tile


def onehot(field, table, product):
    hi, lo = split(field)
    both = product(jnp.concatenate([hi, lo], axis=0), table)
    half = field.shape[0]
    return both[:half] + both[half:]


def weights_of(field):
    hi, lo = split(field)
    return [
        jnp.concatenate([hi[:, h * 128 : h * 128 + 128], lo[:, h * 128 : h * 128 + 128]], axis=1)
        for h in range(2)
    ]


def block_apply(a_hi, a_lo, weights):
    grp = iota((64, 128), 1) // 16
    halves = []
    for h in range(2):
        rows = pl.ds(512 * h, 512)
        w = weights(h)
        one = nn(a_hi[rows, :], w)
        two = nn(a_lo[rows, :], w[:, :128])
        out = one[:, :128] + one[:, 128:] + two
        acc = out[:64]
        for b in range(1, 8):
            acc = jnp.where(grp == b, out[64 * b : 64 * b + 64], acc)
        halves.append(acc)
    return jnp.concatenate(halves, axis=1)


def kernel(
    dims, load_h, mask_h, stiff_h, cols_h, cap_h, pre_h, fmap_h, fw_h, cmap_h, coarse_h,
    x_ref, r_ref,
    load_v, mask_v, stiff_v, cols_v, cap_v, pre_v, fmap_v, fw_v, cmap_v, coarse_v,
    k_hi, k_lo, p_hi, p_lo, cc, table_f, table_c, table_t, fw_rows, fw_full, wk, wc,
    ybuf, gbuf, nbuf, own_a, own_b, red_a, red_b,
    in_sem, y_send, y_recv, g_send, g_recv, a_send, a_recv, b_send, b_recv,
):
    nx, nzl, ny, nzh = dims
    plane, column = nx * ny, nzl * nzh * 2
    dam, sec = lax.axis_index("dam"), lax.axis_index("sec")
    ndam, nsec = nx * nzl * ny, nzh * 2
    xx, zl, yy = dam // (nzl * ny), (dam // ny) % nzl, dam % ny
    zc = ((sec // 2) * nzl + zl) * 2 + sec % 2

    def plane_id(k):
        px, py = (xx + k // ny) % nx, (yy + k % ny) % ny
        return ((px * nzl + zl) * ny + py, sec)

    def column_id(k):
        q = (zc + k) % column
        z = q // 2
        return ((xx * nzl + z % nzl) * ny + yy, (z // nzl) * 2 + q % 2)

    face_ids = (
        ((dam + ndam - 1) % ndam, sec),
        ((dam + 1) % ndam, sec),
        (dam, (sec + nsec - 1) % nsec),
        (dam, (sec + 1) % nsec),
    )

    pairs = (
        (load_h, load_v), (mask_h, mask_v), (cmap_h, cmap_v), (pre_h, pre_v), (coarse_h, coarse_v),
        (fmap_h, fmap_v), (fw_h, fw_v), (cols_h, cols_v), (cap_h, cap_v), (stiff_h, stiff_v),
    )
    loads = [pltpu.make_async_copy(a, b, in_sem.at[n]) for n, (a, b) in enumerate(pairs)]
    for copy in loads:
        copy.start()

    barrier = pltpu.get_barrier_semaphore()

    def greet(target):
        pl.semaphore_signal(barrier, inc=1, device_id=target, device_id_type=MESH)

    greet(face_ids[0])
    greet(face_ids[1])
    lax.fori_loop(1, column, lambda k, c: (greet(column_id(k)), c)[1], 0)
    lax.fori_loop(1, plane, lambda k, c: (greet(plane_id(k)), c)[1], 0)

    lane = iota((8, 128), 1)
    grp8 = lane // 16

    loads[2].wait()
    loads[1].wait()
    loads[0].wait()
    row128 = iota((256, 128), 0)
    lane1, grp1 = iota((1, 128), 1), iota((1, 128), 1) // 16
    corner = cmap_v[...]
    where_c = jnp.zeros((1, 128), i32)
    for n in range(4):
        where_c = jnp.where(
            grp1 % 4 == n, jnp.broadcast_to(corner[:, n : n + 1], (1, 128)), where_c
        )
    target = where_c * 16 + lane1 % 16
    table_c[...] = jnp.where(row128 == jnp.broadcast_to(target, (256, 128)), 1.0, 0.0).astype(bf16)

    fan = jnp.where(iota((16, 128), 1) % 16 == iota((16, 128), 0), 1.0, 0.0)
    mask = nn(mask_v[...].astype(f32), fan)
    halves = []
    for h in range(2):
        m = mask[8 * h : 8 * h + 8]
        halves.append(
            jnp.concatenate(
                [
                    swap8(load_v[pl.ds(8 * h, 8), pl.ds(128 * t, 128)] * m)
                    for t in range(8)
                ],
                axis=0,
            )
        )
    r0 = jnp.concatenate(halves, axis=1)

    low = iota((32, 128), 1) < 64

    def send_corners(rnd, field):
        both = onehot(field, table_c[...], nn)
        ybuf[rnd, sec] = jnp.where(low, both[:32], both[32:])

        def copy(k):
            return pltpu.make_async_remote_copy(
                src_ref=ybuf.at[rnd, sec],
                dst_ref=ybuf.at[rnd, sec],
                send_sem=y_send.at[rnd, k - 1],
                recv_sem=y_recv.at[rnd],
                device_id=(dam, (sec + k) % nsec),
                device_id_type=MESH,
            )

        copies = [copy(k) for k in range(1, nsec)]
        return copies

    def coarse(rnd):
        first, lane32 = iota((32, 128), 1) < 16, None
        for j in range(nsec):
            y = ybuf[rnd, j]
            turned = [y if g == 0 else roll(y, -16 * g, 1) for g in range(8)]
            for n in range(4):
                for dh in range(2):
                    g = dh * 4 + n
                    hi = turned[g].astype(bf16).astype(f32)
                    prev = turned[(g + 7) % 8]
                    lo = prev - prev.astype(bf16).astype(f32)
                    wc[pl.ds(j * 256 + n * 64 + dh * 32, 32), :] = jnp.where(first, hi, lo).astype(bf16)
        out = nn(cc[...], wc[...])
        out = out[:256] + out[256:]
        wide = jnp.concatenate([out[64 * n : 64 * n + 64] for n in range(4)], axis=1)
        return onehot(wide, table_t[...], nt)

    def wait_corners(rnd):
        part = ybuf.at[rnd, pl.ds(0, nsec - 1)]
        pltpu.make_async_copy(part, part, y_recv.at[rnd]).wait()

    def smooth(field):
        w = weights_of(field)
        return block_apply(p_hi, p_lo, lambda h: w[h])

    copies = send_corners(0, r0)
    pl.semaphore_wait(barrier, plane + column)
    for copy in copies:
        copy.start()
    pending = list(copies)

    loads[3].wait()
    for b in range(16):
        hi, lo = split(pre_v[b])
        p_hi[pl.ds(64 * b, 64), :] = hi
        p_lo[pl.ds(64 * b, 64), :] = lo
    z0 = smooth(r0)
    loads[4].wait()
    for n in range(4):
        hi, lo = split(coarse_v[pl.ds(64 * n, 64), :])
        cc[pl.ds(64 * n, 64), :] = hi
        cc[pl.ds(256 + 64 * n, 64), :] = lo
    for n in range(4):
        t = jnp.broadcast_to(corner[:, n : n + 1], (1, 128)) * 16 + lane1 % 16
        t = jnp.where(grp1 < 2, t, -1)
        table_t[:, pl.ds(128 * n, 128)] = jnp.where(
            row128 == jnp.broadcast_to(t, (256, 128)), 1.0, 0.0
        ).astype(bf16)
    loads[5].wait()
    fm = fmap_v[...]
    grp4 = iota((4, 128), 1) // 16
    where_f = jnp.zeros((4, 128), i32)
    for p in range(8):
        where_f = jnp.where(grp4 == p, jnp.broadcast_to(fm[:, p : p + 1], (4, 128)), where_f)
    where_f = where_f * 16 + iota((4, 128), 1) % 16
    for f in range(4):
        table_f[:, pl.ds(128 * f, 128)] = jnp.where(
            row128 == jnp.broadcast_to(where_f[f : f + 1], (256, 128)), 1.0, 0.0
        ).astype(bf16)
    loads[6].wait()
    for f in range(4):
        for p in range(8):
            q = 8 * f + p
            fw_rows[pl.ds(16 * q, 16), :] = jnp.broadcast_to(
                fw_v[f : f + 1, 64 * p : 64 * p + 64], (16, 64)
            )
    eye = jnp.where(iota((64, 64), 0) == iota((64, 64), 1), 1.0, 0.0)
    fw_full[...] = nt(eye, fw_rows[...], HIGH)
    loads[7].wait()
    offsets = [
        jnp.broadcast_to(jnp.broadcast_to(cols_v[k][:, 0:1], (1, 128)), (64, 128)) for k in (1, 3, 5)
    ]
    loads[8].wait()
    place = jnp.where(iota((64, 128), 0) == iota((64, 128), 1), 1.0, 0.0)
    cap = jnp.dot(cap_v[...], place, precision=HIGH, preferred_element_type=f32)
    loads[9].wait()
    on_diag = iota((64, 128), 0) == iota((64, 128), 1)
    for b in range(16):
        rows = pl.ds(64 * b, 64)
        for t in range(4):
            wide = 128 if t < 3 else 64
            piece = stiff_v[b, :, 128 * t : 128 * t + wide]
            if t == 0:
                piece = piece + jnp.where(on_diag, jnp.broadcast_to(cap[b : b + 1], (64, 128)), 0.0)
            hi, lo = split(piece)
            k_hi[rows, 128 * t : 128 * t + wide] = hi
            k_lo[rows, 128 * t : 128 * t + wide] = lo
    k_hi[:, 448:512] = jnp.zeros((1024, 64), bf16)
    k_lo[:, 448:512] = jnp.zeros((1024, 64), bf16)
    for h in range(2):
        wk[h, 448:512, :] = jnp.zeros((64, 256), bf16)

    lane64 = iota((64, 128), 1)

    def shifted(field, bits, sign):
        a, b = field[:, :128], field[:, 128:]
        for s in (1, 2, 4):
            ra, rb = roll(a, -sign * 16 * s, 1), roll(b, -sign * 16 * s, 1)
            same = lane64 < 128 - 16 * s if sign > 0 else lane64 >= 16 * s
            na, nb = jnp.where(same, ra, rb), jnp.where(same, rb, ra)
            on = (bits & s) != 0
            a, b = jnp.where(on, na, a), jnp.where(on, nb, b)
        return jnp.concatenate([a, b], axis=1)

    def send_faces(rnd, field):
        faces = onehot(field, table_f[...], nn)
        out = []
        for f in range(4):
            gbuf[rnd, f] = faces[:, 128 * f : 128 * f + 128]
        for f in (2, 3, 0, 1):
            out.append(
                pltpu.make_async_remote_copy(
                    src_ref=gbuf.at[rnd, f],
                    dst_ref=nbuf.at[rnd, f ^ 1],
                    send_sem=g_send.at[rnd, f],
                    recv_sem=g_recv.at[rnd, f ^ 1],
                    device_id=face_ids[f],
                    device_id_type=MESH,
                )
            )
            out[-1].start()
        return faces, out

    def stiff(field):
        chunks = [field]
        for bits in offsets:
            chunks += [shifted(field, bits, 1), shifted(field, bits, -1)]
        for k, chunk in enumerate(chunks):
            for h, w in enumerate(weights_of(chunk)):
                wk[h, pl.ds(64 * k, 64), :] = w
        return block_apply(k_hi, k_lo, lambda h: wk[h])

    def wait_faces(rnd, faces, copies):
        for copy in copies:
            copy.wait_recv()
        beside = jnp.concatenate([nbuf[rnd, f] for f in range(4)], axis=1)
        return onehot(fw_full[...] * (faces - beside), table_f[...], nt)

    def rows_of(dots):
        sub = iota((8, 128), 0)
        acc = jnp.zeros((8, 128), f32)
        for n, total in enumerate(dots):
            line = total[:, :128] + total[:, 128:]
            line = jnp.sum(line, axis=0, keepdims=True)
            acc = jnp.where(sub == n, jnp.broadcast_to(line, (8, 128)), acc)
        for s in (16, 32, 64):
            acc = acc + roll(acc, s, 1)
        return jnp.sum(jnp.where(sub == grp8, acc, 0.0), axis=0, keepdims=True)

    def exchange(src, dst, send_sem, recv_sem, target, count):
        def body(k, carry):
            pltpu.make_async_remote_copy(
                src_ref=src,
                dst_ref=dst.at[k - 1],
                send_sem=send_sem,
                recv_sem=recv_sem,
                device_id=target(k),
                device_id_type=MESH,
            ).start()
            return carry

        lax.fori_loop(1, count, body, 0)

    def start_sum(rnd, dots):
        own_a[rnd] = rows_of(dots)
        exchange(own_a.at[rnd], red_a.at[rnd], a_send.at[rnd], a_recv.at[rnd], plane_id, plane)

    def relay_sum(rnd):
        pltpu.make_async_copy(red_a.at[rnd], red_a.at[rnd], a_recv.at[rnd]).wait()
        own_b[rnd] = jnp.sum(red_a[rnd], axis=0) + own_a[rnd]
        exchange(own_b.at[rnd], red_b.at[rnd], b_send.at[rnd], b_recv.at[rnd], column_id, column)

    def end_sum(rnd, count):
        pltpu.make_async_copy(red_b.at[rnd], red_b.at[rnd], b_recv.at[rnd]).wait()
        total = jnp.broadcast_to(jnp.sum(red_b[rnd], axis=0) + own_b[rnd], (8, 128))
        sums = []
        for n in range(count):
            one = jnp.where(grp8 == n, total, 0.0)
            for s in (16, 32, 64):
                one = one + roll(one, s, 1)
            sums.append(one)
        return sums

    def wide(coef):
        one = jnp.broadcast_to(coef[0:1], (64, 128))
        return jnp.concatenate([one, one], axis=1)

    wait_corners(0)
    z0 = z0 + coarse(0)
    faces, copies = send_faces(0, z0)
    pending += copies
    w0 = stiff(z0)
    w0 = w0 + wait_faces(0, faces, copies)

    copies = send_corners(1, w0)
    for copy in copies:
        copy.start()
    pending += copies
    start_sum(0, [r0 * z0, z0 * w0])
    q0 = smooth(w0)
    wait_corners(1)
    q0 = q0 + coarse(1)

    faces, copies = send_faces(1, q0)
    pending += copies
    relay_sum(0)
    s0 = stiff(q0)
    s0 = s0 + wait_faces(1, faces, copies)
    gamma, delta = end_sum(0, 2)
    alpha = gamma / delta
    wide_alpha = wide(alpha)
    r1 = r0 - wide_alpha * w0
    z1 = z0 - wide_alpha * q0
    az = w0 - wide_alpha * s0
    start_sum(1, [r1 * z1, z1 * az, z1 * w0 + z0 * az])

    def tiles(field):
        return [
            [swap8(field[8 * t : 8 * t + 8, 128 * h : 128 * h + 128]) for t in range(8)]
            for h in range(2)
        ]

    tz0, tz1 = tiles(z0), tiles(z1)
    relay_sum(1)
    tr1, taz, tw0 = tiles(r1), tiles(az), tiles(w0)
    gnew, e_zz, e_zw = end_sum(1, 3)
    beta = gnew / gamma
    alpha1 = gnew / (e_zz + beta * (e_zw + beta * delta))
    scaled = alpha1 * beta
    for h in range(2):
        for t in range(8):
            at = (pl.ds(8 * h, 8), pl.ds(128 * t, 128))
            x_ref[at] = (alpha + scaled) * tz0[h][t] + alpha1 * tz1[h][t]
            r_ref[at] = tr1[h][t] - alpha1 * taz[h][t] - scaled * tw0[h][t]

    for copy in pending:
        copy.wait_send()
    for rnd in range(2):
        pltpu.make_async_copy(red_a.at[rnd], red_a.at[rnd], a_send.at[rnd]).wait()
        pltpu.make_async_copy(red_b.at[rnd], red_b.at[rnd], b_send.at[rnd]).wait()


def solution(mesh):
    placed = (
        P("dam", "sec", None, None),
        P("dam", "sec", None, None),
        P("dam", "sec", None, None, None),
        P("dam", "sec", None, None),
        P("dam", "sec", None, None),
        P("dam", "sec", None, None, None),
        P("dam", "sec", None, None),
        P("dam", "sec", None, None),
        P("dam", "sec", None),
        P("dam", "sec", None),
    )
    dims = SPLITS[mesh.shape["dam"]] + (mesh.shape["sec"] // 2,)
    nx, nzl, ny, nzh = dims
    plane, column = nx * ny, nzl * nzh * 2

    def shards(load, mask, stiff, cols, cap, pre, fmap, fw, cmap, coarse):
        args = (
            load[0, 0], mask[0, 0], stiff[0, 0], cols[0, 0].T.reshape(7, 1, 16), cap[0, 0],
            pre[0, 0], fmap[0, 0], fw[0, 0], cmap[0], coarse[0],
        )
        vmem = pltpu.VMEM
        dma = pltpu.SemaphoreType.DMA
        scratch = [vmem(a.shape, a.dtype) for a in args] + [
            vmem((1024, 512), bf16), vmem((1024, 512), bf16),
            vmem((1024, 64), bf16), vmem((1024, 64), bf16),
            vmem((512, 1536), bf16),
            vmem((256, 512), bf16), vmem((256, 128), bf16), vmem((256, 512), bf16),
            vmem((512, 64), f32), vmem((64, 512), f32),
            vmem((2, 512, 256), bf16), vmem((1536, 128), bf16),
            vmem((2, 2 * nzh, 32, 128), f32),
            vmem((2, 4, 64, 128), f32), vmem((2, 4, 64, 128), f32),
            vmem((2, 1, 128), f32), vmem((2, 1, 128), f32),
            vmem((2, plane - 1, 1, 128), f32), vmem((2, column - 1, 1, 128), f32),
            dma((10,)),
            dma((2, 2 * nzh - 1)), dma((2,)),
            dma((2, 4)), dma((2, 4)),
            dma((2,)), dma((2,)), dma((2,)), dma((2,)),
        ]
        x, r = pl.pallas_call(
            functools.partial(kernel, dims),
            out_shape=[jax.ShapeDtypeStruct((16, 1024), f32)] * 2,
            in_specs=[pl.BlockSpec(memory_space=pl.ANY)] * 10,
            out_specs=[pl.BlockSpec(memory_space=pltpu.VMEM)] * 2,
            scratch_shapes=scratch,
            compiler_params=pltpu.CompilerParams(
                collective_id=0, has_side_effects=True, vmem_limit_bytes=48 * 1024 * 1024
            ),
        )(*args)
        return x[None, None], r[None, None]

    return jax.shard_map(
        shards,
        mesh=mesh,
        in_specs=placed,
        out_specs=(P("dam", "sec", None, None), P("dam", "sec", None, None)),
        check_vma=False,
    )
```

time: 467 us -> 73 us (0.16)
  blocking collectives: 365 us -> 0 us
  Pallas kernels: 0 us -> 61.6 us
  starting transfers between devices: 30.1 us -> 0 us
  matrix products: 23.9 us -> 0 us
  local copies, waits for them, and re-layouts: 33 us -> 10.3 us
  other arithmetic: 12.8 us -> 0 us
    psum x3 -> x0, blocking collectives: 325 us -> none  [global_inner(): return lax.psum(inner(first, second), ('dam', 'sec'))]
    pallas_call x0 -> x1, Pallas kernels: none -> 61.6 us  [shards(): pl.pallas_call(functools.partial(kernel, dims), out_shape=[jax.ShapeDtype...]
    all_gather x2 -> x0, blocking collectives: 39.6 us -> none  [precondition(): piece = lax.all_gather(corners, 'sec', axis=0, tiled=True)]
    ppermute x8 -> x0, starting transfers between devices: 30.1 us -> none  [the longest x4 22.9 us: with_halo(): before = lax.ppermute(last, axis, up)]
    dot_general x6 -> x0, matrix products: 23.9 us -> none  [the longest x2 15.7 us: local_product(): prod = jnp.einsum('bde,bes->bds', stiff, gathered, precision=HIGH)]
    another operation x15 -> x0, local copies, waits for them, and re-layouts: 13.3 us -> none  [the longest x10 12.2 us: shards(): beside = jnp.stack([dam_side[0], dam_side[3], sec_side[0], sec_side[3]])]
    unnamed x30 -> x21, local copies, waits for them, and re-layouts: 0.65 us -> 10.3 us
    reshape x15 -> x1, local copies, waits for them, and re-layouts: 9.5 us -> 0.01 us  [shards(): cols[0, 0].T.reshape(7, 1, 16)]
  transfers between devices with their start and end apart: 8 -> 0, of which waited for: 0 -> 0; matrix products, arithmetic and copies ran while one was open for 7% -> 0% of each run, Pallas kernels for 0% -> 0%
where the time goes in v1:
time: 73 us; the launch traced here: 72.5 us
  Pallas kernels  61.6 us (84%)
  local copies, waits for them, and re-layouts  10.3 us (14%)
    pallas_call x1, Pallas kernels, shards(): pl.pallas_call(functools.partial(kernel, dims), out_shape=[jax.ShapeDtype...  61.6 us
    unnamed x21, local copies, waits for them, and re-layouts  10.3 us

profile of v1, /device:TPU:1, one launch (start us, length us, event | category | flops | bytes accessed | tf_op | source)
XLA Modules:
  0.0 72.5 jit_solution(16460585139659565033)
XLA Ops:
  0.6 0.7 copy.15
  1.3 0.0 copy-start
  1.3 1.6 %copy-done = f32[1,1,16,64,448]{4,3,2,1,0:T(8,128)S(1)} copy-done((f32[1,1,16,64,448]{4,3,2,1,0:T(8,128)S(1)}, f32[1,1,16,64,448]{4,3,2,1,0:T(8,128)}, u32[]{:S(2)}) %copy-start) | copy-done | bytes 1835032
  2.9 0.0 copy-start.1
  2.9 1.4 %copy-done.1 = f32[1,256,1536]{2,1,0:T(8,128)S(1)} copy-done((f32[1,256,1536]{2,1,0:T(8,128)S(1)}, f32[1,256,1536]{2,1,0:T(8,128)}, u32[]{:S(2)}) %copy-start.1) | copy-done | bytes 1572888
  4.3 0.0 copy-start.2
  4.3 1.0 %copy-done.2 = f32[1,1,16,64,64]{4,3,2,1,0:T(8,128)S(1)} copy-done((f32[1,1,16,64,64]{4,3,2,1,0:T(8,128)S(1)}, f32[1,1,16,64,64]{4,3,2,1,0:T(8,128)}, u32[]{:S(2)}) %copy-start.2) | copy-done | bytes 262168
  5.4 0.0 copy-start.3
  5.4 0.8 %copy-done.3 = f32[1,1,16,1024]{3,2,1,0:T(8,128)S(1)} copy-done((f32[1,1,16,1024]{3,2,1,0:T(8,128)S(1)}, f32[1,1,16,1024]{3,2,1,0:T(8,128)}, u32[]{:S(2)}) %copy-start.3) | copy-done | bytes 65560
  6.2 0.0 copy-start.4
  6.2 0.7 copy-done.4
  6.9 0.0 copy-start.5
  6.9 0.7 copy-done.5
  7.6 0.0 copy-start.6
  7.6 0.7 copy-done.6
  8.3 0.0 copy-start.7
  8.3 0.7 copy-done.7
  9.0 0.0 copy-start.8
  9.0 0.7 copy-done.8
  9.6 61.6 %shard_map.113 = (f32[16,1024]{1,0:T(8,128)S(1)}, f32[16,1024]{1,0:T(8,128)S(1)}) custom-call(f32[16,1024]{1,0:T(8,128)S(1)} %bitcast.21, s32[16,16]{1,0:T(8,128)S(1)} %bitcast.24, f32[16,64,448]{2,1,0:T(8,128)S(1)} %bitcast.18, s32[7,1,16]{2,1,0:T(1,128)S(1)} %copy.12.cols_h, f32[16,64]{1,0:T(8,128)S(1)} %bitcast.25, f32[16,64,64]{2,1,0:T(8,128)S(1)} %bitcast.20, ...), custom_call_target="tpu_custom_call" | custom-call | tf_op jit(solution)/shard_map/pallas_call | solution.py:463
  71.2 0.6 copy.18
  71.9 0.6 copy.19
  (1 shorter events, 0.0 us)
Async XLA Ops:
  1.3 1.6 %copy-start = (f32[1,1,16,64,448]{4,3,2,1,0:T(8,128)S(1)}, f32[1,1,16,64,448]{4,3,2,1,0:T(8,128)}, u32[]{:S(2)}) copy-start(f32[1,1,16,64,448]{4,3,2,1,0:T(8,128)} %param.12) | copy-start | bytes 5505028
  2.9 1.4 %copy-start.1 = (f32[1,256,1536]{2,1,0:T(8,128)S(1)}, f32[1,256,1536]{2,1,0:T(8,128)}, u32[]{:S(2)}) copy-start(f32[1,256,1536]{2,1,0:T(8,128)} %param.19) | copy-start | bytes 4718596
  4.3 1.0 %copy-start.2 = (f32[1,1,16,64,64]{4,3,2,1,0:T(8,128)S(1)}, f32[1,1,16,64,64]{4,3,2,1,0:T(8,128)}, u32[]{:S(2)}) copy-start(f32[1,1,16,64,64]{4,3,2,1,0:T(8,128)} %param.15) | copy-start | bytes 786436
  5.4 0.8 %copy-start.3 = (f32[1,1,16,1024]{3,2,1,0:T(8,128)S(1)}, f32[1,1,16,1024]{3,2,1,0:T(8,128)}, u32[]{:S(2)}) copy-start(f32[1,1,16,1024]{3,2,1,0:T(8,128)} %param.10) | copy-start | bytes 196612
  6.2 0.7 copy-start.4
  6.9 0.7 copy-start.5
  7.6 0.7 copy-start.6
  8.3 0.7 copy-start.7
  9.0 0.7 copy-start.8

commit v2 on v1

--- a/solution.py
+++ b/solution.py
@@ -79,9 +79,9 @@
 
 def kernel(
     dims, load_h, mask_h, stiff_h, cols_h, cap_h, pre_h, fmap_h, fw_h, cmap_h, coarse_h,
-    x_ref, r_ref,
+    out_ref,
     load_v, mask_v, stiff_v, cols_v, cap_v, pre_v, fmap_v, fw_v, cmap_v, coarse_v,
-    k_hi, k_lo, p_hi, p_lo, cc, table_f, table_c, table_t, fw_rows, fw_full, wk, wc,
+    k_hi, k_lo, p_hi, p_lo, cc, table_f, table_c, table_t, table_tf, table_fc, fw_rows, fw_full, wk, wc,
     ybuf, gbuf, nbuf, own_a, own_b, red_a, red_b,
     in_sem, y_send, y_recv, g_send, g_recv, a_send, a_recv, b_send, b_recv,
 ):
@@ -113,7 +113,7 @@
         (fmap_h, fmap_v), (fw_h, fw_v), (cols_h, cols_v), (cap_h, cap_v), (stiff_h, stiff_v),
     )
     loads = [pltpu.make_async_copy(a, b, in_sem.at[n]) for n, (a, b) in enumerate(pairs)]
-    for copy in loads:
+    for copy in loads[:3]:
         copy.start()
 
     barrier = pltpu.get_barrier_semaphore()
@@ -121,10 +121,15 @@
     def greet(target):
         pl.semaphore_signal(barrier, inc=1, device_id=target, device_id_type=MESH)
 
-    greet(face_ids[0])
-    greet(face_ids[1])
-    lax.fori_loop(1, column, lambda k, c: (greet(column_id(k)), c)[1], 0)
-    lax.fori_loop(1, plane, lambda k, c: (greet(plane_id(k)), c)[1], 0)
+    below, above = dam > 0, dam < ndam - 1
+    column_ids = [column_id(k) for k in range(1, column)]
+    plane_ids = [plane_id(k) for k in range(1, plane)]
+    for target in column_ids + plane_ids:
+        greet(target)
+    pl.when(below)(lambda: greet(face_ids[0]))
+    pl.when(above)(lambda: greet(face_ids[1]))
+    for copy in loads[3:]:
+        copy.start()
 
     lane = iota((8, 128), 1)
     grp8 = lane // 16
@@ -160,28 +165,32 @@
     r0 = jnp.concatenate(halves, axis=1)
 
     low = iota((32, 128), 1) < 64
-
-    def send_corners(rnd, field):
-        both = onehot(field, table_c[...], nn)
-        ybuf[rnd, sec] = jnp.where(low, both[:32], both[32:])
-
-        def copy(k):
+    zh, core = sec // 2, sec % 2
+
+    def corner_copies(rnd):
+        def copy(dz, rc):
             return pltpu.make_async_remote_copy(
                 src_ref=ybuf.at[rnd, sec],
                 dst_ref=ybuf.at[rnd, sec],
-                send_sem=y_send.at[rnd, k - 1],
-                recv_sem=y_recv.at[rnd],
-                device_id=(dam, (sec + k) % nsec),
+                send_sem=y_send.at[rnd, 2 * dz + rc - 1],
+                recv_sem=y_recv.at[rnd, dz],
+                device_id=(dam, ((zh + dz) % nzh) * 2 + (core + rc) % 2),
                 device_id_type=MESH,
             )
 
-        copies = [copy(k) for k in range(1, nsec)]
-        return copies
-
-    def coarse(rnd):
-        first, lane32 = iota((32, 128), 1) < 16, None
-        for j in range(nsec):
-            y = ybuf[rnd, j]
+        return [copy(dz, rc) for dz in range(1, nzh) for rc in range(2)] + [copy(0, 1)]
+
+    def put_corners(rnd, both):
+        ybuf[rnd, sec] = jnp.where(low, both[:32], both[32:])
+
+    def coarse_part(rnd, dz):
+        count = 2 if dz else 1
+        part = ybuf.at[rnd, pl.ds(0, count)]
+        pltpu.make_async_copy(part, part, y_recv.at[rnd, dz]).wait()
+        chip = (zh + nzh - dz) % nzh
+        first = iota((32, 128), 1) < 16
+        for c in range(2):
+            y = ybuf[rnd, 2 * chip + c]
             turned = [y if g == 0 else roll(y, -16 * g, 1) for g in range(8)]
             for n in range(4):
                 for dh in range(2):
@@ -189,22 +198,27 @@
                     hi = turned[g].astype(bf16).astype(f32)
                     prev = turned[(g + 7) % 8]
                     lo = prev - prev.astype(bf16).astype(f32)
-                    wc[pl.ds(j * 256 + n * 64 + dh * 32, 32), :] = jnp.where(first, hi, lo).astype(bf16)
-        out = nn(cc[...], wc[...])
+                    wc[dz, pl.ds(c * 256 + n * 64 + dh * 32, 32), :] = jnp.where(first, hi, lo).astype(bf16)
+        return nn(cc[:, pl.ds(pl.multiple_of(chip * 512, 512), 512)], wc[dz])
+
+    def coarse_rest(rnd, out):
+        for dz in range(1, nzh):
+            out = out + coarse_part(rnd, dz)
         out = out[:256] + out[256:]
         wide = jnp.concatenate([out[64 * n : 64 * n + 64] for n in range(4)], axis=1)
-        return onehot(wide, table_t[...], nt)
-
-    def wait_corners(rnd):
-        part = ybuf.at[rnd, pl.ds(0, nsec - 1)]
-        pltpu.make_async_copy(part, part, y_recv.at[rnd]).wait()
+        hi, lo = split(wide)
+        return jnp.concatenate([hi, lo], axis=0)
+
+    def fold(both):
+        return both[:64] + both[64:]
 
     def smooth(field):
         w = weights_of(field)
         return block_apply(p_hi, p_lo, lambda h: w[h])
 
-    copies = send_corners(0, r0)
-    pl.semaphore_wait(barrier, plane + column)
+    put_corners(0, onehot(r0, table_c[...], nn))
+    copies = corner_copies(0)
+    pl.semaphore_wait(barrier, plane + column - 2 + below.astype(i32) + above.astype(i32))
     for copy in copies:
         copy.start()
     pending = list(copies)
@@ -237,6 +251,22 @@
         table_f[:, pl.ds(128 * f, 128)] = jnp.where(
             row128 == jnp.broadcast_to(where_f[f : f + 1], (256, 128)), 1.0, 0.0
         ).astype(bf16)
+    modrow = iota((128, 128), 0) % 16
+    rown = (iota((128, 128), 0) // 16) % 4
+    early = iota((128, 128), 0) < 32
+    for f in range(4):
+        lanes = where_f[f : f + 1]
+        match = jnp.zeros((128, 128), i32)
+        for n in range(4):
+            t = jnp.where(
+                lanes // 16 == jnp.broadcast_to(corner[:, n : n + 1], (1, 128)), lane1 % 16, -1
+            )
+            t = jnp.broadcast_to(t, (128, 128))
+            match = jnp.where(rown == n, t, match)
+            table_tf[pl.ds(128 * n, 128), pl.ds(128 * f, 128)] = jnp.where(
+                early, jnp.where(modrow == t, 1.0, 0.0), 0.0
+            ).astype(bf16)
+        table_fc[:, pl.ds(128 * f, 128)] = jnp.where(modrow == match, 1.0, 0.0).astype(bf16)
     loads[6].wait()
     for f in range(4):
         for p in range(8):
@@ -282,24 +312,23 @@
             a, b = jnp.where(on, na, a), jnp.where(on, nb, b)
         return jnp.concatenate([a, b], axis=1)
 
-    def send_faces(rnd, field):
-        faces = onehot(field, table_f[...], nn)
-        out = []
+    def face_copy(rnd, f):
+        return pltpu.make_async_remote_copy(
+            src_ref=gbuf.at[rnd, f],
+            dst_ref=nbuf.at[rnd, f ^ 1],
+            send_sem=g_send.at[rnd, f],
+            recv_sem=g_recv.at[rnd, f ^ 1],
+            device_id=face_ids[f],
+            device_id_type=MESH,
+        )
+
+    def send_faces(rnd, faces):
         for f in range(4):
             gbuf[rnd, f] = faces[:, 128 * f : 128 * f + 128]
-        for f in (2, 3, 0, 1):
-            out.append(
-                pltpu.make_async_remote_copy(
-                    src_ref=gbuf.at[rnd, f],
-                    dst_ref=nbuf.at[rnd, f ^ 1],
-                    send_sem=g_send.at[rnd, f],
-                    recv_sem=g_recv.at[rnd, f ^ 1],
-                    device_id=face_ids[f],
-                    device_id_type=MESH,
-                )
-            )
-            out[-1].start()
-        return faces, out
+        face_copy(rnd, 2).start()
+        face_copy(rnd, 3).start()
+        pl.when(below)(lambda: face_copy(rnd, 0).start())
+        pl.when(above)(lambda: face_copy(rnd, 1).start())
 
     def stiff(field):
         chunks = [field]
@@ -310,11 +339,14 @@
                 wk[h, pl.ds(64 * k, 64), :] = w
         return block_apply(k_hi, k_lo, lambda h: wk[h])
 
-    def wait_faces(rnd, faces, copies):
-        for copy in copies:
-            copy.wait_recv()
+    def wait_faces(rnd, faces):
+        pl.when(above)(lambda: face_copy(rnd, 0).wait_recv())
+        pl.when(below)(lambda: face_copy(rnd, 1).wait_recv())
+        face_copy(rnd, 2).wait_recv()
+        face_copy(rnd, 3).wait_recv()
         beside = jnp.concatenate([nbuf[rnd, f] for f in range(4)], axis=1)
-        return onehot(fw_full[...] * (faces - beside), table_f[...], nt)
+        hi, lo = split(fw_full[...] * (faces - beside))
+        return jnp.concatenate([hi, lo], axis=0)
 
     def rows_of(dots):
         sub = iota((8, 128), 0)
@@ -327,28 +359,25 @@
             acc = acc + roll(acc, s, 1)
         return jnp.sum(jnp.where(sub == grp8, acc, 0.0), axis=0, keepdims=True)
 
-    def exchange(src, dst, send_sem, recv_sem, target, count):
-        def body(k, carry):
+    def exchange(src, dst, send_sem, recv_sem, targets):
+        for k, target in enumerate(targets):
             pltpu.make_async_remote_copy(
                 src_ref=src,
-                dst_ref=dst.at[k - 1],
+                dst_ref=dst.at[k],
                 send_sem=send_sem,
                 recv_sem=recv_sem,
-                device_id=target(k),
+                device_id=target,
                 device_id_type=MESH,
             ).start()
-            return carry
-
-        lax.fori_loop(1, count, body, 0)
 
     def start_sum(rnd, dots):
         own_a[rnd] = rows_of(dots)
-        exchange(own_a.at[rnd], red_a.at[rnd], a_send.at[rnd], a_recv.at[rnd], plane_id, plane)
+        exchange(own_a.at[rnd], red_a.at[rnd], a_send.at[rnd], a_recv.at[rnd], plane_ids)
 
     def relay_sum(rnd):
         pltpu.make_async_copy(red_a.at[rnd], red_a.at[rnd], a_recv.at[rnd]).wait()
         own_b[rnd] = jnp.sum(red_a[rnd], axis=0) + own_a[rnd]
-        exchange(own_b.at[rnd], red_b.at[rnd], b_send.at[rnd], b_recv.at[rnd], column_id, column)
+        exchange(own_b.at[rnd], red_b.at[rnd], b_send.at[rnd], b_recv.at[rnd], column_ids)
 
     def end_sum(rnd, count):
         pltpu.make_async_copy(red_b.at[rnd], red_b.at[rnd], b_recv.at[rnd]).wait()
@@ -365,34 +394,49 @@
         one = jnp.broadcast_to(coef[0:1], (64, 128))
         return jnp.concatenate([one, one], axis=1)
 
-    wait_corners(0)
-    z0 = z0 + coarse(0)
-    faces, copies = send_faces(0, z0)
-    pending += copies
+    def clear(f):
+        for rnd in range(2):
+            nbuf[rnd, f] = jnp.zeros((64, 128), f32)
+
+    pl.when(dam == 0)(lambda: clear(0))
+    pl.when(dam == ndam - 1)(lambda: clear(1))
+
+    faces = onehot(z0, table_f[...], nn)
+    part = coarse_part(0, 0)
+    fix = coarse_rest(0, part)
+    faces = faces + fold(nn(fix, table_tf[...]))
+    send_faces(0, faces)
+    z0 = z0 + fold(nt(fix, table_t[...]))
     w0 = stiff(z0)
-    w0 = w0 + wait_faces(0, faces, copies)
-
-    copies = send_corners(1, w0)
+    corners = onehot(w0, table_c[...], nn)
+    term = wait_faces(0, faces)
+    put_corners(1, corners + fold(nt(term, table_fc[...])))
+    copies = corner_copies(1)
     for copy in copies:
         copy.start()
     pending += copies
+    w0 = w0 + fold(nt(term, table_f[...]))
+
     start_sum(0, [r0 * z0, z0 * w0])
     q0 = smooth(w0)
-    wait_corners(1)
-    q0 = q0 + coarse(1)
-
-    faces, copies = send_faces(1, q0)
-    pending += copies
+    faces = onehot(q0, table_f[...], nn)
+    part = coarse_part(1, 0)
+    fix = coarse_rest(1, part)
+    faces = faces + fold(nn(fix, table_tf[...]))
+    send_faces(1, faces)
     relay_sum(0)
+
+    q0 = q0 + fold(nt(fix, table_t[...]))
     s0 = stiff(q0)
-    s0 = s0 + wait_faces(1, faces, copies)
     gamma, delta = end_sum(0, 2)
     alpha = gamma / delta
     wide_alpha = wide(alpha)
     r1 = r0 - wide_alpha * w0
     z1 = z0 - wide_alpha * q0
-    az = w0 - wide_alpha * s0
-    start_sum(1, [r1 * z1, z1 * az, z1 * w0 + z0 * az])
+    rz, zw = r1 * z1, z1 * w0
+    term = wait_faces(1, faces)
+    az = w0 - wide_alpha * (s0 + fold(nt(term, table_f[...])))
+    start_sum(1, [rz, z1 * az, zw + z0 * az])
 
     def tiles(field):
         return [
@@ -410,11 +454,16 @@
     for h in range(2):
         for t in range(8):
             at = (pl.ds(8 * h, 8), pl.ds(128 * t, 128))
-            x_ref[at] = (alpha + scaled) * tz0[h][t] + alpha1 * tz1[h][t]
-            r_ref[at] = tr1[h][t] - alpha1 * taz[h][t] - scaled * tw0[h][t]
+            out_ref[(0,) + at] = (alpha + scaled) * tz0[h][t] + alpha1 * tz1[h][t]
+            out_ref[(1,) + at] = tr1[h][t] - alpha1 * taz[h][t] - scaled * tw0[h][t]
 
     for copy in pending:
         copy.wait_send()
+    for rnd in range(2):
+        face_copy(rnd, 2).wait_send()
+        face_copy(rnd, 3).wait_send()
+        pl.when(below)(lambda: face_copy(rnd, 0).wait_send())
+        pl.when(above)(lambda: face_copy(rnd, 1).wait_send())
     for rnd in range(2):
         pltpu.make_async_copy(red_a.at[rnd], red_a.at[rnd], a_send.at[rnd]).wait()
         pltpu.make_async_copy(red_b.at[rnd], red_b.at[rnd], b_send.at[rnd]).wait()
@@ -439,7 +488,7 @@
 
     def shards(load, mask, stiff, cols, cap, pre, fmap, fw, cmap, coarse):
         args = (
-            load[0, 0], mask[0, 0], stiff[0, 0], cols[0, 0].T.reshape(7, 1, 16), cap[0, 0],
+            load[0, 0], mask[0, 0], stiff[0, 0], cols.transpose(0, 3, 1, 2)[0], cap[0, 0],
             pre[0, 0], fmap[0, 0], fw[0, 0], cmap[0], coarse[0],
         )
         vmem = pltpu.VMEM
@@ -449,28 +498,29 @@
             vmem((1024, 64), bf16), vmem((1024, 64), bf16),
             vmem((512, 1536), bf16),
             vmem((256, 512), bf16), vmem((256, 128), bf16), vmem((256, 512), bf16),
+            vmem((512, 512), bf16), vmem((128, 512), bf16),
             vmem((512, 64), f32), vmem((64, 512), f32),
-            vmem((2, 512, 256), bf16), vmem((1536, 128), bf16),
+            vmem((2, 512, 256), bf16), vmem((3, 512, 128), bf16),
             vmem((2, 2 * nzh, 32, 128), f32),
             vmem((2, 4, 64, 128), f32), vmem((2, 4, 64, 128), f32),
             vmem((2, 1, 128), f32), vmem((2, 1, 128), f32),
             vmem((2, plane - 1, 1, 128), f32), vmem((2, column - 1, 1, 128), f32),
             dma((10,)),
-            dma((2, 2 * nzh - 1)), dma((2,)),
+            dma((2, 2 * nzh - 1)), dma((2, nzh)),
             dma((2, 4)), dma((2, 4)),
             dma((2,)), dma((2,)), dma((2,)), dma((2,)),
         ]
-        x, r = pl.pallas_call(
+        out = pl.pallas_call(
             functools.partial(kernel, dims),
-            out_shape=[jax.ShapeDtypeStruct((16, 1024), f32)] * 2,
+            out_shape=jax.ShapeDtypeStruct((2, 16, 1024), f32),
             in_specs=[pl.BlockSpec(memory_space=pl.ANY)] * 10,
-            out_specs=[pl.BlockSpec(memory_space=pltpu.VMEM)] * 2,
+            out_specs=pl.BlockSpec(memory_space=pltpu.VMEM),
             scratch_shapes=scratch,
             compiler_params=pltpu.CompilerParams(
-                collective_id=0, has_side_effects=True, vmem_limit_bytes=48 * 1024 * 1024
+                collective_id=0, has_side_effects=True, vmem_limit_bytes=67043328
             ),
         )(*args)
-        return x[None, None], r[None, None]
+        return out[0][None, None], out[1][None, None]
 
     return jax.shard_map(
         shards,

time: 73 us -> 64.3 us (0.88)
  local copies, waits for them, and re-layouts: 10.3 us -> 1.53 us
    unnamed x21 -> x0, local copies, waits for them, and re-layouts: 10.3 us -> none
    another operation x0 -> x1, local copies, waits for them, and re-layouts: none -> 1.53 us  [shards(): return (out[0][None, None], out[1][None, None])]
where the time goes in v2:
time: 64.3 us; the launch traced here: 64.1 us
  Pallas kernels  62 us (96%)
  local copies, waits for them, and re-layouts  1.53 us (2%)
    pallas_call x1, Pallas kernels, shards(): pl.pallas_call(functools.partial(kernel, dims), out_shape=jax.ShapeDtypeS...  62 us
    another operation x1, local copies, waits for them, and re-layouts, shards(): return (out[0][None, None], out[1][None, None])  1.53 us

profile of v2, /device:TPU:1, one launch (start us, length us, event | category | flops | bytes accessed | tf_op | source)
XLA Modules:
  0.0 64.1 jit_solution(8235963398876584972)
XLA Ops:
  0.6 62.0 %shard_map.113 = f32[2,16,1024]{2,1,0:T(8,128)} custom-call(f32[16,1024]{1,0:T(8,128)} %bitcast.19, s32[16,16]{1,0:T(8,128)} %bitcast.20, f32[16,64,448]{2,1,0:T(8,128)} %bitcast.16, s32[7,1,16]{2,1,0:T(1,128)} %bitcast.23, f32[16,64]{1,0:T(8,128)} %bitcast.21, f32[16,64,64]{2,1,0:T(8,128)} %bitcast.18, s32[4,8]{1,0:T(4,128)} %bitcast.24, ...), custom_call_target="tpu_custom_call" | custom-call | tf_op jit(solution)/shard_map/pallas_call | solution.py:513
  62.6 1.5 %slice_bitcast_fusion = (f32[1,1,16,1024]{3,2,1,0:T(8,128)}, f32[1,1,16,1024]{3,2,1,0:T(8,128)}) fusion(f32[2,16,1024]{2,1,0:T(8,128)} %shard_map.113), kind=kLoop, calls=%fused_computation | loop fusion | bytes 262144 | tf_op jit(solution)/shard_map/broadcast_in_dim;squeeze | solution.py:523

commit v3 on v2

--- a/solution.py
+++ b/solution.py
@@ -82,30 +82,32 @@
     out_ref,
     load_v, mask_v, stiff_v, cols_v, cap_v, pre_v, fmap_v, fw_v, cmap_v, coarse_v,
     k_hi, k_lo, p_hi, p_lo, cc, table_f, table_c, table_t, table_tf, table_fc, fw_rows, fw_full, wk, wc,
-    ybuf, gbuf, nbuf, own_a, own_b, red_a, red_b,
+    ybuf, gbuf, nbuf, own_a, own_b, red_a, red_b, fields, turned,
     in_sem, y_send, y_recv, g_send, g_recv, a_send, a_recv, b_send, b_recv,
 ):
     nx, nzl, ny, nzh = dims
     plane, column = nx * ny, nzl * nzh * 2
     dam, sec = lax.axis_index("dam"), lax.axis_index("sec")
     ndam, nsec = nx * nzl * ny, nzh * 2
-    xx, zl, yy = dam // (nzl * ny), (dam // ny) % nzl, dam % ny
-    zc = ((sec // 2) * nzl + zl) * 2 + sec % 2
-
-    def plane_id(k):
-        px, py = (xx + k // ny) % nx, (yy + k % ny) % ny
-        return ((px * nzl + zl) * ny + py, sec)
-
-    def column_id(k):
-        q = (zc + k) % column
-        z = q // 2
-        return ((xx * nzl + z % nzl) * ny + yy, (z // nzl) * 2 + q % 2)
+    xx, zl, yy = lax.div(dam, nzl * ny), lax.rem(lax.div(dam, ny), nzl), lax.rem(dam, ny)
+    zh, core = lax.div(sec, 2), lax.rem(sec, 2)
+
+    def turns(at, size):
+        return [at] + [jnp.where(at + k < size, at + k, at + k - size) for k in range(1, size)]
+
+    ring_y, ring_core = turns(yy, ny), turns(core, 2)
+    ring_x = [x * (nzl * ny) for x in turns(xx, nx)]
+    ring_zl, ring_zh = [z * ny for z in turns(zl, nzl)], [z * 2 for z in turns(zh, nzh)]
+    plane_ids = [(x + zl * ny + y, sec) for x in ring_x for y in ring_y][1:]
+    column_ids = [
+        (ring_x[0] + z + yy, h + c) for h in ring_zh for z in ring_zl for c in ring_core
+    ][1:]
 
     face_ids = (
-        ((dam + ndam - 1) % ndam, sec),
-        ((dam + 1) % ndam, sec),
-        (dam, (sec + nsec - 1) % nsec),
-        (dam, (sec + 1) % nsec),
+        (jnp.where(dam > 0, dam - 1, ndam - 1), sec),
+        (jnp.where(dam < ndam - 1, dam + 1, 0), sec),
+        (dam, jnp.where(sec > 0, sec - 1, nsec - 1)),
+        (dam, jnp.where(sec < nsec - 1, sec + 1, 0)),
     )
 
     pairs = (
@@ -122,8 +124,6 @@
         pl.semaphore_signal(barrier, inc=1, device_id=target, device_id_type=MESH)
 
     below, above = dam > 0, dam < ndam - 1
-    column_ids = [column_id(k) for k in range(1, column)]
-    plane_ids = [plane_id(k) for k in range(1, plane)]
     for target in column_ids + plane_ids:
         greet(target)
     pl.when(below)(lambda: greet(face_ids[0]))
@@ -165,7 +165,6 @@
     r0 = jnp.concatenate(halves, axis=1)
 
     low = iota((32, 128), 1) < 64
-    zh, core = sec // 2, sec % 2
 
     def corner_copies(rnd):
         def copy(dz, rc):
@@ -174,7 +173,7 @@
                 dst_ref=ybuf.at[rnd, sec],
                 send_sem=y_send.at[rnd, 2 * dz + rc - 1],
                 recv_sem=y_recv.at[rnd, dz],
-                device_id=(dam, ((zh + dz) % nzh) * 2 + (core + rc) % 2),
+                device_id=(dam, ring_zh[dz] + ring_core[rc]),
                 device_id_type=MESH,
             )
 
@@ -183,11 +182,8 @@
     def put_corners(rnd, both):
         ybuf[rnd, sec] = jnp.where(low, both[:32], both[32:])
 
-    def coarse_part(rnd, dz):
-        count = 2 if dz else 1
-        part = ybuf.at[rnd, pl.ds(0, count)]
-        pltpu.make_async_copy(part, part, y_recv.at[rnd, dz]).wait()
-        chip = (zh + nzh - dz) % nzh
+    def coarse_weights(rnd, dz):
+        chip = zh if dz == 0 else lax.div(ring_zh[nzh - dz], 2)
         first = iota((32, 128), 1) < 16
         for c in range(2):
             y = ybuf[rnd, 2 * chip + c]
@@ -199,12 +195,24 @@
                     prev = turned[(g + 7) % 8]
                     lo = prev - prev.astype(bf16).astype(f32)
                     wc[dz, pl.ds(c * 256 + n * 64 + dh * 32, 32), :] = jnp.where(first, hi, lo).astype(bf16)
-        return nn(cc[:, pl.ds(pl.multiple_of(chip * 512, 512), 512)], wc[dz])
+        return pl.ds(pl.multiple_of(chip * 512, 512), 512)
+
+    def wait_corners(rnd, dz):
+        part = ybuf.at[rnd, pl.ds(0, 2 if dz else 1)]
+        pltpu.make_async_copy(part, part, y_recv.at[rnd, dz]).wait()
+
+    def coarse_own(rnd):
+        wait_corners(rnd, 0)
+        at = coarse_weights(rnd, 0)
+        return nn(cc[:256, at], wc[0]) + nn(cc[256:, at], wc[0])
 
     def coarse_rest(rnd, out):
         for dz in range(1, nzh):
-            out = out + coarse_part(rnd, dz)
-        out = out[:256] + out[256:]
+            wait_corners(rnd, dz)
+        at = [coarse_weights(rnd, dz) for dz in range(1, nzh)]
+        parts = [nn(cc[:256, a], wc[n + 1]) for n, a in enumerate(at)]
+        parts += [nn(cc[256:, a], wc[n + 1]) for n, a in enumerate(at)]
+        out = out + sum(parts[1:], parts[0])
         wide = jnp.concatenate([out[64 * n : 64 * n + 64] for n in range(4)], axis=1)
         hi, lo = split(wide)
         return jnp.concatenate([hi, lo], axis=0)
@@ -345,15 +353,21 @@
         face_copy(rnd, 2).wait_recv()
         face_copy(rnd, 3).wait_recv()
         beside = jnp.concatenate([nbuf[rnd, f] for f in range(4)], axis=1)
-        hi, lo = split(fw_full[...] * (faces - beside))
-        return jnp.concatenate([hi, lo], axis=0)
+        return fw_full[...] * (faces - beside)
+
+    def two(value):
+        return jnp.concatenate(split(value), axis=0)
+
+    def lump(prod):
+        line = sum(prod[:, 128 * n : 128 * n + 128] for n in range(1, prod.shape[1] // 128))
+        line = prod[:, :128] + line
+        return sum((line[8 * t : 8 * t + 8] for t in range(1, 8)), line[:8])
 
     def rows_of(dots):
         sub = iota((8, 128), 0)
         acc = jnp.zeros((8, 128), f32)
         for n, total in enumerate(dots):
-            line = total[:, :128] + total[:, 128:]
-            line = jnp.sum(line, axis=0, keepdims=True)
+            line = jnp.sum(total, axis=0, keepdims=True)
             acc = jnp.where(sub == n, jnp.broadcast_to(line, (8, 128)), acc)
         for s in (16, 32, 64):
             acc = acc + roll(acc, s, 1)
@@ -402,14 +416,14 @@
     pl.when(dam == ndam - 1)(lambda: clear(1))
 
     faces = onehot(z0, table_f[...], nn)
-    part = coarse_part(0, 0)
+    part = coarse_own(0)
     fix = coarse_rest(0, part)
     faces = faces + fold(nn(fix, table_tf[...]))
     send_faces(0, faces)
     z0 = z0 + fold(nt(fix, table_t[...]))
     w0 = stiff(z0)
     corners = onehot(w0, table_c[...], nn)
-    term = wait_faces(0, faces)
+    term = two(wait_faces(0, faces))
     put_corners(1, corners + fold(nt(term, table_fc[...])))
     copies = corner_copies(1)
     for copy in copies:
@@ -417,10 +431,10 @@
     pending += copies
     w0 = w0 + fold(nt(term, table_f[...]))
 
-    start_sum(0, [r0 * z0, z0 * w0])
+    start_sum(0, [lump(r0 * z0), lump(z0 * w0)])
     q0 = smooth(w0)
     faces = onehot(q0, table_f[...], nn)
-    part = coarse_part(1, 0)
+    part = coarse_own(1)
     fix = coarse_rest(1, part)
     faces = faces + fold(nn(fix, table_tf[...]))
     send_faces(1, faces)
@@ -433,20 +447,27 @@
     wide_alpha = wide(alpha)
     r1 = r0 - wide_alpha * w0
     z1 = z0 - wide_alpha * q0
-    rz, zw = r1 * z1, z1 * w0
-    term = wait_faces(1, faces)
-    az = w0 - wide_alpha * (s0 + fold(nt(term, table_f[...])))
-    start_sum(1, [rz, z1 * az, zw + z0 * az])
-
-    def tiles(field):
-        return [
-            [swap8(field[8 * t : 8 * t + 8, 128 * h : 128 * h + 128]) for t in range(8)]
-            for h in range(2)
-        ]
-
-    tz0, tz1 = tiles(z0), tiles(z1)
+    az = w0 - wide_alpha * s0
+    face_alpha = jnp.concatenate([wide_alpha, wide_alpha], axis=1)
+    faces_z = jnp.concatenate([gbuf[0, f] for f in range(4)], axis=1)
+    faces_z1 = faces_z - face_alpha * faces
+    rz, zz, zw = lump(r1 * z1), lump(z1 * az), lump(z1 * w0 + z0 * az)
+    term = face_alpha * wait_faces(1, faces)
+    start_sum(1, [rz, zz - lump(faces_z1 * term), zw - lump(faces_z * term)])
+
+    @pl.when(dam >= 0)
+    def _():
+        fields[0], fields[1], fields[2], fields[4] = z0, z1, r1, w0
+        fields[3] = az - fold(nt(two(term), table_f[...]))
+
+    def turn(t, carry):
+        for n in range(5):
+            for h in range(2):
+                turned[n, h, t] = swap8(fields[n, pl.ds(pl.multiple_of(8 * t, 8), 8), 128 * h : 128 * h + 128])
+        return carry
+
+    lax.fori_loop(0, 8, turn, 0)
     relay_sum(1)
-    tr1, taz, tw0 = tiles(r1), tiles(az), tiles(w0)
     gnew, e_zz, e_zw = end_sum(1, 3)
     beta = gnew / gamma
     alpha1 = gnew / (e_zz + beta * (e_zw + beta * delta))
@@ -454,8 +475,8 @@
     for h in range(2):
         for t in range(8):
             at = (pl.ds(8 * h, 8), pl.ds(128 * t, 128))
-            out_ref[(0,) + at] = (alpha + scaled) * tz0[h][t] + alpha1 * tz1[h][t]
-            out_ref[(1,) + at] = tr1[h][t] - alpha1 * taz[h][t] - scaled * tw0[h][t]
+            out_ref[(0,) + at] = (alpha + scaled) * turned[0, h, t] + alpha1 * turned[1, h, t]
+            out_ref[(1,) + at] = turned[2, h, t] - alpha1 * turned[3, h, t] - scaled * turned[4, h, t]
 
     for copy in pending:
         copy.wait_send()
@@ -505,6 +526,7 @@
             vmem((2, 4, 64, 128), f32), vmem((2, 4, 64, 128), f32),
             vmem((2, 1, 128), f32), vmem((2, 1, 128), f32),
             vmem((2, plane - 1, 1, 128), f32), vmem((2, column - 1, 1, 128), f32),
+            vmem((5, 64, 256), f32), vmem((5, 2, 8, 8, 128), f32),
             dma((10,)),
             dma((2, 2 * nzh - 1)), dma((2, nzh)),
             dma((2, 4)), dma((2, 4)),

time: 64.3 us -> 61.4 us (0.955)
  Pallas kernels: 62 us -> 59 us
    pallas_call x1, Pallas kernels: 62 us -> 59 us  [shards(): pl.pallas_call(functools.partial(kernel, dims), out_shape=jax.ShapeDtypeS...]
where the time goes in v3:
time: 61.4 us; the launch traced here: 61.1 us
  Pallas kernels  59 us (96%)
  local copies, waits for them, and re-layouts  1.53 us (2%)
  between operations  0.64 us (1%)
    pallas_call x1, Pallas kernels, shards(): pl.pallas_call(functools.partial(kernel, dims), out_shape=jax.ShapeDtypeS...  59 us
    another operation x1, local copies, waits for them, and re-layouts, shards(): return (out[0][None, None], out[1][None, None])  1.53 us

profile of v3, /device:TPU:1, one launch (start us, length us, event | category | flops | bytes accessed | tf_op | source)
XLA Modules:
  0.0 61.1 jit_solution(56724043440891729)
XLA Ops:
  0.6 59.0 %shard_map.113 = f32[2,16,1024]{2,1,0:T(8,128)} custom-call(f32[16,1024]{1,0:T(8,128)} %bitcast.19, s32[16,16]{1,0:T(8,128)} %bitcast.20, f32[16,64,448]{2,1,0:T(8,128)} %bitcast.16, s32[7,1,16]{2,1,0:T(1,128)} %bitcast.23, f32[16,64]{1,0:T(8,128)} %bitcast.21, f32[16,64,64]{2,1,0:T(8,128)} %bitcast.18, s32[4,8]{1,0:T(4,128)} %bitcast.24, ...), custom_call_target="tpu_custom_call" | custom-call | tf_op jit(solution)/shard_map/pallas_call | solution.py:535
  59.6 1.5 %slice_bitcast_fusion = (f32[1,1,16,1024]{3,2,1,0:T(8,128)}, f32[1,1,16,1024]{3,2,1,0:T(8,128)}) fusion(f32[2,16,1024]{2,1,0:T(8,128)} %shard_map.113), kind=kLoop, calls=%fused_computation | loop fusion | bytes 262144 | tf_op jit(solution)/shard_map/broadcast_in_dim;squeeze | solution.py:545

commit v4 on v3

--- a/solution.py
+++ b/solution.py
@@ -83,7 +83,7 @@
     load_v, mask_v, stiff_v, cols_v, cap_v, pre_v, fmap_v, fw_v, cmap_v, coarse_v,
     k_hi, k_lo, p_hi, p_lo, cc, table_f, table_c, table_t, table_tf, table_fc, fw_rows, fw_full, wk, wc,
     ybuf, gbuf, nbuf, own_a, own_b, red_a, red_b, fields, turned,
-    in_sem, y_send, y_recv, g_send, g_recv, a_send, a_recv, b_send, b_recv,
+    in_sem, y_send, y_recv, g_send, g_recv, a_send, a_recv, b_send, b_recv, word,
 ):
     nx, nzl, ny, nzh = dims
     plane, column = nx * ny, nzl * nzh * 2
@@ -97,11 +97,24 @@
 
     ring_y, ring_core = turns(yy, ny), turns(core, 2)
     ring_x = [x * (nzl * ny) for x in turns(xx, nx)]
-    ring_zl, ring_zh = [z * ny for z in turns(zl, nzl)], [z * 2 for z in turns(zh, nzh)]
-    plane_ids = [(x + zl * ny + y, sec) for x in ring_x for y in ring_y][1:]
-    column_ids = [
-        (ring_x[0] + z + yy, h + c) for h in ring_zh for z in ring_zl for c in ring_core
-    ][1:]
+    ring_zh = [z * 2 for z in turns(zh, nzh)]
+    nz = nzh * nzl
+
+    def far(k, size):
+        return min(k, size - k)
+
+    order = sorted(
+        ((kx, ky) for kx in range(nx) for ky in range(ny)),
+        key=lambda k: -far(k[0], nx) - far(k[1], ny),
+    )[:-1]
+    plane_ids = [(ring_x[kx] + zl * ny + ring_y[ky], sec) for kx, ky in order]
+    column_ids = []
+    ring_z = turns(zh * nzl + zl, nz)
+    for k in sorted(range(nz), key=lambda k: -far(k, nz)):
+        high = sum(jnp.where(ring_z[k] >= nzl * n, 1, 0) for n in range(1, nzh))
+        along = ring_x[0] + (ring_z[k] - high * nzl) * ny + yy
+        column_ids += [(along, high * 2 + c) for c in ring_core]
+    column_ids = column_ids[:-2] + column_ids[-1:]
 
     face_ids = (
         (jnp.where(dam > 0, dam - 1, ndam - 1), sec),
@@ -124,7 +137,14 @@
         pl.semaphore_signal(barrier, inc=1, device_id=target, device_id_type=MESH)
 
     below, above = dam > 0, dam < ndam - 1
-    for target in column_ids + plane_ids:
+    row, base = ring_x[0] + zl * ny, zl * ny + yy
+    ring_l = [z * ny for z in turns(zl, nzl)]
+    beside_y = [(row + ring_y[1], sec), (row + ring_y[-1], sec)]
+    beside_x = [(ring_x[1] + base, sec), (ring_x[-1] + base, sec)]
+    beside_l = [(ring_x[0] + ring_l[1] + yy, sec), (ring_x[0] + ring_l[-1] + yy, sec)]
+    peers = [(dam, h + c) for h in ring_zh for c in ring_core][1:]
+    near = peers[::-1] + beside_l + beside_x + beside_y
+    for target in near:
         greet(target)
     pl.when(below)(lambda: greet(face_ids[0]))
     pl.when(above)(lambda: greet(face_ids[1]))
@@ -226,10 +246,19 @@
 
     put_corners(0, onehot(r0, table_c[...], nn))
     copies = corner_copies(0)
-    pl.semaphore_wait(barrier, plane + column - 2 + below.astype(i32) + above.astype(i32))
+    pl.semaphore_wait(barrier, len(near) + below.astype(i32) + above.astype(i32))
     for copy in copies:
         copy.start()
-    pending = list(copies)
+
+    def tell(n, targets):
+        for target in targets:
+            pl.semaphore_signal(word.at[n], inc=1, device_id=target, device_id_type=MESH)
+
+    def hear(n, count):
+        pl.semaphore_wait(word.at[n], count)
+
+    tell(0, beside_y)
+    tell(5, beside_l)
 
     loads[3].wait()
     for b in range(16):
@@ -275,6 +304,10 @@
                 early, jnp.where(modrow == t, 1.0, 0.0), 0.0
             ).astype(bf16)
         table_fc[:, pl.ds(128 * f, 128)] = jnp.where(modrow == match, 1.0, 0.0).astype(bf16)
+    hear(0, 2)
+    tell(1, beside_y)
+    hear(5, 2)
+    tell(6, beside_l[:1])
     loads[6].wait()
     for f in range(4):
         for p in range(8):
@@ -408,6 +441,9 @@
         one = jnp.broadcast_to(coef[0:1], (64, 128))
         return jnp.concatenate([one, one], axis=1)
 
+    hear(1, 2)
+    tell(2, beside_y)
+
     def clear(f):
         for rnd in range(2):
             nbuf[rnd, f] = jnp.zeros((64, 128), f32)
@@ -420,17 +456,22 @@
     fix = coarse_rest(0, part)
     faces = faces + fold(nn(fix, table_tf[...]))
     send_faces(0, faces)
+    hear(2, 2)
+    tell(3, beside_x)
     z0 = z0 + fold(nt(fix, table_t[...]))
     w0 = stiff(z0)
     corners = onehot(w0, table_c[...], nn)
+    hear(3, 2)
+    tell(4, beside_x[:1])
     term = two(wait_faces(0, faces))
     put_corners(1, corners + fold(nt(term, table_fc[...])))
     copies = corner_copies(1)
     for copy in copies:
         copy.start()
-    pending += copies
     w0 = w0 + fold(nt(term, table_f[...]))
 
+    hear(4, 1)
+    hear(6, 1)
     start_sum(0, [lump(r0 * z0), lump(z0 * w0)])
     q0 = smooth(w0)
     faces = onehot(q0, table_f[...], nn)
@@ -467,6 +508,15 @@
         return carry
 
     lax.fori_loop(0, 8, turn, 0)
+    for rnd in range(2):
+        for copy in corner_copies(rnd):
+            copy.wait_send()
+        face_copy(rnd, 2).wait_send()
+        face_copy(rnd, 3).wait_send()
+        pl.when(below)(lambda: face_copy(rnd, 0).wait_send())
+        pl.when(above)(lambda: face_copy(rnd, 1).wait_send())
+    pltpu.make_async_copy(red_a.at[0], red_a.at[0], a_send.at[0]).wait()
+    pltpu.make_async_copy(red_b.at[0], red_b.at[0], b_send.at[0]).wait()
     relay_sum(1)
     gnew, e_zz, e_zw = end_sum(1, 3)
     beta = gnew / gamma
@@ -478,16 +528,8 @@
             out_ref[(0,) + at] = (alpha + scaled) * turned[0, h, t] + alpha1 * turned[1, h, t]
             out_ref[(1,) + at] = turned[2, h, t] - alpha1 * turned[3, h, t] - scaled * turned[4, h, t]
 
-    for copy in pending:
-        copy.wait_send()
-    for rnd in range(2):
-        face_copy(rnd, 2).wait_send()
-        face_copy(rnd, 3).wait_send()
-        pl.when(below)(lambda: face_copy(rnd, 0).wait_send())
-        pl.when(above)(lambda: face_copy(rnd, 1).wait_send())
-    for rnd in range(2):
-        pltpu.make_async_copy(red_a.at[rnd], red_a.at[rnd], a_send.at[rnd]).wait()
-        pltpu.make_async_copy(red_b.at[rnd], red_b.at[rnd], b_send.at[rnd]).wait()
+    pltpu.make_async_copy(red_a.at[1], red_a.at[1], a_send.at[1]).wait()
+    pltpu.make_async_copy(red_b.at[1], red_b.at[1], b_send.at[1]).wait()
 
 
 def solution(mesh):
@@ -531,6 +573,7 @@
             dma((2, 2 * nzh - 1)), dma((2, nzh)),
             dma((2, 4)), dma((2, 4)),
             dma((2,)), dma((2,)), dma((2,)), dma((2,)),
+            pltpu.SemaphoreType.REGULAR((7,)),
         ]
         out = pl.pallas_call(
             functools.partial(kernel, dims),

time: 61.4 us -> 59.2 us (0.964)
  Pallas kernels: 59 us -> 56.9 us
    pallas_call x1, Pallas kernels: 59 us -> 56.9 us  [shards(): pl.pallas_call(functools.partial(kernel, dims), out_shape=jax.ShapeDtypeS...]
where the time goes in v4:
time: 59.2 us; the launch traced here: 59 us
  Pallas kernels  56.9 us (96%)
  local copies, waits for them, and re-layouts  1.53 us (3%)
  between operations  0.64 us (1%)
    pallas_call x1, Pallas kernels, shards(): pl.pallas_call(functools.partial(kernel, dims), out_shape=jax.ShapeDtypeS...  56.9 us
    another operation x1, local copies, waits for them, and re-layouts, shards(): return (out[0][None, None], out[1][None, None])  1.53 us

profile of v4, /device:TPU:1, one launch (start us, length us, event | category | flops | bytes accessed | tf_op | source)
XLA Modules:
  0.0 59.0 jit_solution(17104662206664412623)
XLA Ops:
  0.6 56.9 %shard_map.113 = f32[2,16,1024]{2,1,0:T(8,128)} custom-call(f32[16,1024]{1,0:T(8,128)} %bitcast.19, s32[16,16]{1,0:T(8,128)} %bitcast.20, f32[16,64,448]{2,1,0:T(8,128)} %bitcast.16, s32[7,1,16]{2,1,0:T(1,128)} %bitcast.23, f32[16,64]{1,0:T(8,128)} %bitcast.21, f32[16,64,64]{2,1,0:T(8,128)} %bitcast.18, s32[4,8]{1,0:T(4,128)} %bitcast.24, ...), custom_call_target="tpu_custom_call" | custom-call | tf_op jit(solution)/shard_map/pallas_call | solution.py:578
  57.5 1.5 %slice_bitcast_fusion = (f32[1,1,16,1024]{3,2,1,0:T(8,128)}, f32[1,1,16,1024]{3,2,1,0:T(8,128)}) fusion(f32[2,16,1024]{2,1,0:T(8,128)} %shard_map.113), kind=kLoop, calls=%fused_computation | loop fusion | bytes 262144 | tf_op jit(solution)/shard_map/broadcast_in_dim;squeeze | solution.py:588

commit v5 on v4

--- a/solution.py
+++ b/solution.py
@@ -83,7 +83,7 @@
     load_v, mask_v, stiff_v, cols_v, cap_v, pre_v, fmap_v, fw_v, cmap_v, coarse_v,
     k_hi, k_lo, p_hi, p_lo, cc, table_f, table_c, table_t, table_tf, table_fc, fw_rows, fw_full, wk, wc,
     ybuf, gbuf, nbuf, own_a, own_b, red_a, red_b, fields, turned,
-    in_sem, y_send, y_recv, g_send, g_recv, a_send, a_recv, b_send, b_recv, word,
+    in_sem, y_send, y_recv, g_recv, a_send, a_recv, b_send, b_recv, word,
 ):
     nx, nzl, ny, nzh = dims
     plane, column = nx * ny, nzl * nzh * 2
@@ -98,24 +98,6 @@
     ring_y, ring_core = turns(yy, ny), turns(core, 2)
     ring_x = [x * (nzl * ny) for x in turns(xx, nx)]
     ring_zh = [z * 2 for z in turns(zh, nzh)]
-    nz = nzh * nzl
-
-    def far(k, size):
-        return min(k, size - k)
-
-    order = sorted(
-        ((kx, ky) for kx in range(nx) for ky in range(ny)),
-        key=lambda k: -far(k[0], nx) - far(k[1], ny),
-    )[:-1]
-    plane_ids = [(ring_x[kx] + zl * ny + ring_y[ky], sec) for kx, ky in order]
-    column_ids = []
-    ring_z = turns(zh * nzl + zl, nz)
-    for k in sorted(range(nz), key=lambda k: -far(k, nz)):
-        high = sum(jnp.where(ring_z[k] >= nzl * n, 1, 0) for n in range(1, nzh))
-        along = ring_x[0] + (ring_z[k] - high * nzl) * ny + yy
-        column_ids += [(along, high * 2 + c) for c in ring_core]
-    column_ids = column_ids[:-2] + column_ids[-1:]
-
     face_ids = (
         (jnp.where(dam > 0, dam - 1, ndam - 1), sec),
         (jnp.where(dam < ndam - 1, dam + 1, 0), sec),
@@ -230,9 +212,9 @@
         for dz in range(1, nzh):
             wait_corners(rnd, dz)
         at = [coarse_weights(rnd, dz) for dz in range(1, nzh)]
-        parts = [nn(cc[:256, a], wc[n + 1]) for n, a in enumerate(at)]
-        parts += [nn(cc[256:, a], wc[n + 1]) for n, a in enumerate(at)]
-        out = out + sum(parts[1:], parts[0])
+        w = jnp.concatenate([wc[dz] for dz in range(1, nzh)], axis=0)
+        for rows in (pl.ds(0, 256), pl.ds(256, 256)):
+            out = out + nn(jnp.concatenate([cc[rows, a] for a in at], axis=1), w)
         wide = jnp.concatenate([out[64 * n : 64 * n + 64] for n in range(4)], axis=1)
         hi, lo = split(wide)
         return jnp.concatenate([hi, lo], axis=0)
@@ -259,6 +241,24 @@
 
     tell(0, beside_y)
     tell(5, beside_l)
+
+    nz = nzh * nzl
+
+    def far(k, size):
+        return min(k, size - k)
+
+    order = sorted(
+        ((kx, ky) for kx in range(nx) for ky in range(ny)),
+        key=lambda k: -far(k[0], nx) - far(k[1], ny),
+    )[:-1]
+    plane_ids = [(ring_x[kx] + zl * ny + ring_y[ky], sec) for kx, ky in order]
+    column_ids = []
+    ring_z = turns(zh * nzl + zl, nz)
+    for k in sorted(range(nz), key=lambda k: -far(k, nz)):
+        high = sum(jnp.where(ring_z[k] >= nzl * n, 1, 0) for n in range(1, nzh))
+        along = ring_x[0] + (ring_z[k] - high * nzl) * ny + yy
+        column_ids += [(along, high * 2 + c) for c in ring_core]
+    column_ids = column_ids[:-2] + column_ids[-1:]
 
     loads[3].wait()
     for b in range(16):
@@ -357,7 +357,7 @@
         return pltpu.make_async_remote_copy(
             src_ref=gbuf.at[rnd, f],
             dst_ref=nbuf.at[rnd, f ^ 1],
-            send_sem=g_send.at[rnd, f],
+            send_sem=in_sem.at[4 * rnd + f],
             recv_sem=g_recv.at[rnd, f ^ 1],
             device_id=face_ids[f],
             device_id_type=MESH,
@@ -571,7 +571,7 @@
             vmem((5, 64, 256), f32), vmem((5, 2, 8, 8, 128), f32),
             dma((10,)),
             dma((2, 2 * nzh - 1)), dma((2, nzh)),
-            dma((2, 4)), dma((2, 4)),
+            dma((2, 4)),
             dma((2,)), dma((2,)), dma((2,)), dma((2,)),
             pltpu.SemaphoreType.REGULAR((7,)),
         ]

time: 59.2 us -> 59.1 us (level)
  no operation moved by 1% of the time
where the time goes in v5:
time: 59.1 us; the launch traced here: 58.9 us
  Pallas kernels  56.8 us (96%)
  local copies, waits for them, and re-layouts  1.53 us (3%)
  between operations  0.64 us (1%)
    pallas_call x1, Pallas kernels, shards(): pl.pallas_call(functools.partial(kernel, dims), out_shape=jax.ShapeDtypeS...  56.8 us
    another operation x1, local copies, waits for them, and re-layouts, shards(): return (out[0][None, None], out[1][None, None])  1.53 us

profile of v5, /device:TPU:1, one launch (start us, length us, event | category | flops | bytes accessed | tf_op | source)
XLA Modules:
  0.0 58.9 jit_solution(11621520601006893019)
XLA Ops:
  0.6 56.8 %shard_map.113 = f32[2,16,1024]{2,1,0:T(8,128)} custom-call(f32[16,1024]{1,0:T(8,128)} %bitcast.19, s32[16,16]{1,0:T(8,128)} %bitcast.20, f32[16,64,448]{2,1,0:T(8,128)} %bitcast.16, s32[7,1,16]{2,1,0:T(1,128)} %bitcast.23, f32[16,64]{1,0:T(8,128)} %bitcast.21, f32[16,64,64]{2,1,0:T(8,128)} %bitcast.18, s32[4,8]{1,0:T(4,128)} %bitcast.24, ...), custom_call_target="tpu_custom_call" | custom-call | tf_op jit(solution)/shard_map/pallas_call | solution.py:578
  57.4 1.5 %slice_bitcast_fusion = (f32[1,1,16,1024]{3,2,1,0:T(8,128)}, f32[1,1,16,1024]{3,2,1,0:T(8,128)}) fusion(f32[2,16,1024]{2,1,0:T(8,128)} %shard_map.113), kind=kLoop, calls=%fused_computation | loop fusion | bytes 262144 | tf_op jit(solution)/shard_map/broadcast_in_dim;squeeze | solution.py:588
